TPU v7x, 32 devices: a whole 2x2x4 slice. The times are simulated.
32 devices in a mesh: rep: 8 (over z, core), seq: 4 (over y, x).
Axes of the slice: x: 2, y: 2, z: 4, core: 2. Of those that a mesh axis runs over, the one named last changes fastest.
Arguments:
- tokens_in: bfloat16 [8, 512, 1536], P('rep', 'seq'), may hold values from -6 to 6
- qkv_weight: bfloat16 [8, 1536, 1024], P('rep'), may hold values from -6 to 6
- out_cotangent: bfloat16 [8, 512, 768], P('rep', 'seq'), may hold values from -24 to 24
- step_index: int32 [1], replicated, may hold values from 0 to 1023
Outputs:
- mixed_weight: float32 [8, 1536, 1024], P('rep', 'seq')
- input_grad: bfloat16 [8, 512, 1536], P('rep', 'seq')
All inputs are finite; a program needn't handle non-finite values.
Results may differ from a plain program's by a relative error of at most 0.02.
The roundings to bfloat16 on the way count: a program that leaves them out, or rounds other values in their place, can miss the bound.
Values may be sent and summed in bfloat16 or wider, within the bound.
No kernel may reach another device: no remote copies, remote signals or barrier semaphores. Data moves between devices by JAX's collectives and lax.ppermute only.
A program may use at most 64 MiB of HBM per device.

v0:
```python
import jax
import jax.numpy as jnp
from jax import lax
from jax.experimental import pallas as pl
from jax.experimental.pallas import tpu as pltpu
from jax.sharding import PartitionSpec as P


DH = 128
WINDOW = 1024
LEARN_RATE = 2.0
MASKED = -1e30
LOG2E = 1.4426950408889634
F32 = jnp.float32
BF16 = jnp.bfloat16
VMEM = pltpu.MemorySpace.VMEM
SMEM = pltpu.MemorySpace.SMEM
HBM = pltpu.MemorySpace.HBM
GRANT = 16 << 20
SPLIT = {0: (6,), 1: (4, 2), 2: (3, 1, 2)}


def xor_pairs(size, key):
    return [(i, i ^ key) for i in range(size)]


def dot(a, b, ca, cb):
    return lax.dot_general(a, b, (((ca,), (cb,)), ((), ())), preferred_element_type=F32)


def local_call(body, args, shapes, scalars=0, **kwargs):
    specs = [
        pl.BlockSpec(memory_space=SMEM if i < scalars else VMEM) for i in range(len(args))
    ]
    args = [
        a if i < scalars else pltpu.with_memory_space_constraint(a, VMEM)
        for i, a in enumerate(args)
    ]
    return pl.pallas_call(
        body,
        out_shape=[VMEM(s, d) for s, d in shapes],
        in_specs=specs,
        out_specs=[pl.BlockSpec(memory_space=VMEM)] * len(shapes),
        compiler_params=pltpu.CompilerParams(vmem_limit_bytes=GRANT),
        **kwargs,
    )(*args)


def kv_project(tokens, weight, heads_dim, scale):
    rows, width = tokens.shape
    cols = weight.shape[1] - heads_dim
    steps = 1
    depth = width // steps

    def body(x_ref, w_ref, o_ref, t_ref, held, sems):
        copies = []
        for i in range(steps):
            span = pl.ds(i * depth, depth)
            one = pltpu.make_async_copy(x_ref.at[:, span], t_ref.at[:, span], sems.at[0, i])
            two = pltpu.make_async_copy(
                w_ref.at[span, heads_dim : heads_dim + cols], held.at[span], sems.at[1, i]
            )
            one.start()
            two.start()
            copies.append((one, two))
        total = None
        for i, (one, two) in enumerate(copies):
            one.wait()
            two.wait()
            span = slice(i * depth, (i + 1) * depth)
            part = dot(t_ref[:, span], held[span, :], 1, 0)
            total = part if total is None else total + part
        o_ref[...] = (total * scale).astype(BF16)

    return pl.pallas_call(
        body,
        out_shape=[VMEM((rows, cols), BF16), VMEM((rows, width), BF16)],
        in_specs=[pl.BlockSpec(memory_space=pl.ANY)] * 2,
        out_specs=[pl.BlockSpec(memory_space=VMEM)] * 2,
        scratch_shapes=[pltpu.VMEM((width, cols), BF16), pltpu.SemaphoreType.DMA((2, steps))],
        compiler_params=pltpu.CompilerParams(vmem_limit_bytes=GRANT),
        name="kv_project",
    )(*[pltpu.with_memory_space_constraint(a, HBM) for a in (tokens, weight)])


def q_project(tokens, weight, cols, scale, place_of, slices, share):
    rows = tokens.shape[0]

    def body(x_ref, w_ref, o_ref, *outs):
        for k, t_ref in enumerate(outs):
            start = pl.multiple_of(place_of(k) * share, 128)
            t_ref[...] = x_ref[:, pl.ds(start, share)]
        o_ref[...] = (dot(x_ref[...], w_ref[:, :cols], 1, 0) * scale).astype(BF16)

    shapes = [((rows, cols), BF16)] + [((rows, share), BF16)] * slices
    return local_call(body, [tokens, weight], shapes)


def attention(place_of, queries, cotangent, blocks, carried, first, heads, last, packed):
    rows = queries.shape[0]
    count = len(blocks)
    cols = heads * DH
    kv = 2 * DH
    group = 2
    scale = DH ** (-0.5)
    factor = scale * LOG2E
    packed = packed and last
    args = [queries, cotangent] + list(blocks)
    if carried is not None:
        args.append(carried)

    def body(*refs):
        q_ref, g_ref = refs[0], refs[1]
        b_refs = refs[2 : 2 + count]
        outs = refs[len(args) :]
        k_all = jnp.concatenate([b[:, :DH] for b in b_refs], axis=0)
        v_all = jnp.concatenate([b[:, DH:] for b in b_refs], axis=0)
        base = lax.broadcasted_iota(jnp.int32, (rows, rows), 1) - lax.broadcasted_iota(
            jnp.int32, (rows, rows), 0
        )
        place = place_of(0)
        bias = []
        for j in range(count):
            origin = place_of(j)
            spread = base + (place - origin) * rows
            ok = (spread >= 0) & (spread < WINDOW) & (origin >= 0)
            bias.append(jnp.where(ok, 0.0, MASKED))
        bias = jnp.concatenate(bias, axis=0)
        total = None
        for h in range(first, first + heads, group):
            span = range(h, min(h + group, first + heads))
            q = jnp.concatenate([q_ref[:, j * DH : (j + 1) * DH] for j in span], axis=0)
            g = jnp.concatenate([g_ref[:, j * DH : (j + 1) * DH] for j in span], axis=0)
            s = dot(k_all, q, 1, 1) + jnp.concatenate([bias] * len(span), axis=1)
            peak = jnp.max(s, axis=0, keepdims=True)
            e = jnp.exp2((s - peak) * factor)
            p = e * (1.0 / jnp.sum(e, axis=0, keepdims=True))
            r = p.astype(BF16)
            dp = dot(v_all, g, 1, 1)
            delta = jnp.sum(r.astype(F32) * dp, axis=0, keepdims=True)
            ds = (p * (dp - delta) * scale).astype(BF16)
            dq = dot(ds, k_all, 0, 0).astype(BF16)
            for n, j in enumerate(span):
                at = (j - first) * DH
                piece = dq[n * rows : (n + 1) * rows]
                outs[0][:, at : at + DH] = piece
                if packed:
                    for o_ref in outs[2:]:
                        o_ref[:, at : at + DH] = piece
            part = jnp.concatenate([dot(ds, q, 1, 0), dot(r, g, 1, 0)], axis=1)
            total = part if total is None else total + part
        if carried is not None:
            total = total + refs[2 + count][...]
        if not last:
            outs[1][...] = total
        else:
            outs[1][...] = total[:rows]
            for j in range(1, count):
                part = total[j * rows : (j + 1) * rows].astype(BF16)
                if packed:
                    outs[1 + j][:, cols:] = part
                else:
                    outs[1 + j][...] = part

    shapes = [((rows, cols), BF16)]
    if not last:
        shapes.append(((count * rows, kv), F32))
    else:
        shapes.append(((rows, kv), F32))
        width = cols + kv if packed else kv
        shapes += [((rows, width), BF16)] * (count - 1)
    return local_call(body, args, shapes)


def turned(step_index, columns):
    tokens, share = sum(a.shape[0] for a in columns), columns[0].shape[1]

    def body(s_ref, *refs):
        x_ref, rate_ref = refs[-2:]
        at = 0
        for ref in refs[:-2]:
            n = ref.shape[0]
            x_ref[:, at : at + n] = ref[...].T
            at += n
        rate = LEARN_RATE * (1.0 + s_ref[0].astype(F32) / 1024.0)
        rate_ref[...] = jnp.full(rate_ref.shape, rate, F32)

    shapes = [((share, tokens), BF16), ((8, 128), F32)]
    return local_call(body, [step_index] + list(columns), shapes, scalars=1)


def update(rate, columns, grads, weight, first, share, scale):
    cols = grads[0][2]

    def body(rate_ref, x_ref, *refs):
        w_ref, u_ref, b_ref = refs[-3:]
        g = jnp.concatenate([r[:, at : at + n] for r, (_, at, n) in zip(refs, grads)], axis=0)
        start = pl.multiple_of(lax.axis_index("seq") * share, share)
        w = w_ref[pl.ds(start, share), first : first + cols].astype(F32)
        step = jnp.concatenate([rate_ref[:1, :]] * (cols // 128), axis=1)
        u = w - step * (dot(x_ref[...], g, 1, 0) * scale)
        u_ref[...] = u
        b_ref[...] = u.astype(BF16)

    return local_call(
        body,
        [rate, columns] + [a for a, _, _ in grads] + [weight],
        [((share, cols), F32), ((share, cols), BF16)],
    )


def average(target, chunks, width):
    share = chunks[0][0].shape[0]
    pieces = 3 if share % 48 == 0 else 1
    step = share // pieces
    total = sum(u.shape[1] for u, _, _ in chunks)

    def body(*refs):
        o_ref, buffer, sems = refs[-3:]
        copies = []
        at = 0
        for i, (u, _, first) in enumerate(chunks):
            u_ref, p_ref = refs[2 * i], refs[2 * i + 1]
            cols = u.shape[1]
            for n in range(pieces):
                span = slice(n * step, (n + 1) * step)
                mean = 0.5 * (u_ref[span, :] + p_ref[span, :].astype(F32))
                buffer[span, at : at + cols] = mean
                copy = pltpu.make_async_copy(
                    buffer.at[span, at : at + cols],
                    o_ref.at[span, first : first + cols],
                    sems.at[i, n],
                )
                copy.start()
                copies.append(copy)
            at += cols
        for copy in copies:
            copy.wait()

    args = [pltpu.with_memory_space_constraint(a, VMEM) for u, p, _ in chunks for a in (u, p)]
    specs = [pl.BlockSpec(memory_space=VMEM)] * len(args)
    alias = {}
    if target is not None:
        alias = {len(args): 0}
        args.append(pltpu.with_memory_space_constraint(target, HBM))
        specs.append(pl.BlockSpec(memory_space=pl.ANY))
    return pl.pallas_call(
        body,
        out_shape=HBM((share, width), F32),
        in_specs=specs,
        out_specs=pl.BlockSpec(memory_space=pl.ANY),
        scratch_shapes=[
            pltpu.VMEM((share, total), F32),
            pltpu.SemaphoreType.DMA((len(chunks), pieces)),
        ],
        input_output_aliases=alias,
        compiler_params=pltpu.CompilerParams(vmem_limit_bytes=GRANT),
    )(*args)


def marker(array):
    def body(x_ref, o_ref):
        o_ref[...] = x_ref[:8, :128].astype(F32)

    return local_call(body, [array], [((8, 128), F32)])[0]


def pair_total(own, arrived, mark):
    rows, kv = own.shape

    def body(*refs):
        total = refs[0][...]
        for ref, (_, at) in zip(refs[1:], arrived):
            total = total + ref[:, at : at + kv].astype(F32)
        refs[-1][...] = total.astype(BF16)

    args = [own] + [a for a, _ in arrived] + ([] if mark is None else [mark])
    return local_call(body, args, [((rows, kv), BF16)])[0]


def input_part(pieces, weight):
    rows, cols = pieces[0].shape[0], sum(p.shape[1] for p in pieces)

    def body(*refs):
        w_ref, o_ref = refs[-2:]
        g = jnp.concatenate([r[...] for r in refs[:-2]], axis=1)
        o_ref[...] = dot(g, w_ref[:, :cols], 1, 1)

    shapes = [((rows, weight.shape[0]), F32)]
    return local_call(body, list(pieces) + [weight], shapes)[0]


def input_gradient(part, piece, weight, scale):
    rows, cols = piece.shape
    width = weight.shape[0]

    def body(part_ref, g_ref, w_ref, o_ref, held, sem):
        total = part_ref[...] + dot(g_ref[...], w_ref[:, -cols:], 1, 1)
        held[...] = (total * scale).astype(BF16)
        copy = pltpu.make_async_copy(held, o_ref, sem)
        copy.start()
        copy.wait()

    args = [pltpu.with_memory_space_constraint(a, VMEM) for a in (part, piece, weight)]
    return pl.pallas_call(
        body,
        out_shape=HBM((rows, width), BF16),
        in_specs=[pl.BlockSpec(memory_space=VMEM)] * len(args),
        out_specs=pl.BlockSpec(memory_space=pl.ANY),
        scratch_shapes=[pltpu.VMEM((rows, width), BF16), pltpu.SemaphoreType.DMA(())],
        compiler_params=pltpu.CompilerParams(vmem_limit_bytes=GRANT),
        name="input_gradient",
    )(*args)


def step(tokens, weight, cotangent, step_index, bit):
    rows, width = tokens.shape
    heads_dim = cotangent.shape[1]
    heads = heads_dim // DH
    kv = weight.shape[1] - heads_dim
    scale = width ** (-0.5)
    parts = lax.axis_size("seq")
    share = width // parts
    hops = min(-(-(WINDOW + rows - 1) // rows) - 1, parts - 1)
    pairwise = hops == parts - 1 and parts in (2, 4) and share % 128 == 0
    others = range(1, parts)
    near = range(1, hops + 1)

    def place_of(hop):
        place = lax.axis_index("seq")
        return place ^ hop if pairwise else place - hop

    def swap(array, key):
        return lax.ppermute(array, "seq", xor_pairs(parts, key))

    def shift(array, hop):
        pairs = [(i, i + hop) for i in range(parts) if 0 <= i + hop < parts]
        return lax.ppermute(array, "seq", pairs)

    def gather(array):
        return lax.all_gather(array, "seq", axis=0, tiled=True)

    def partner(array):
        return lax.ppermute(array, "rep", xor_pairs(lax.axis_size("rep"), 1 << bit))

    def exchange(array, hop):
        return swap(array, abs(hop)) if pairwise else shift(array, hop)

    own_kv, held = kv_project(tokens, weight, heads_dim, scale)
    weight, own_kv = lax.optimization_barrier((weight, own_kv))
    blocks = [own_kv] + [exchange(own_kv, k) for k in near]
    slices = parts if pairwise else 0
    res = q_project(held, weight, heads_dim, scale, place_of, slices, share)
    queries = res[0]
    if pairwise:
        columns = [res[1]] + [swap(res[1 + k], k) for k in others]
    else:
        stacked = tokens.reshape(rows, parts, share).transpose(1, 0, 2)
        stacked = lax.all_to_all(stacked, "seq", 0, 0, tiled=False)
        columns = [stacked.reshape(parts * rows, share)]

    columns, rate = turned(step_index, columns)
    split = SPLIT[min(bit, 2)]
    if sum(split) != heads:
        split = (heads,)
    tags = "abd"[: len(split)]
    alone = len(split) == 1
    cols = [n * DH for n in split]
    pieces, grads = [], []
    carried, first = None, 0
    for tag, n in zip(tags, split):
        last = first + n == heads
        packed = pairwise and last and not alone
        res = attention(place_of, queries, cotangent, blocks, carried, first, n, last, packed)
        pieces.append(res[0])
        if last and not packed:
            partials = [exchange(res[1 + k], -k) for k in near]
            arrived = [(a, 0) for a in partials]
        if packed:
            packs = [swap(res[1 + k], k) for k in others]
            grads.append([(a, 0, n * DH) for a in [res[0]] + packs])
            arrived = [(a, n * DH) for a in packs]
        elif pairwise:
            moved = [swap(res[0], k) for k in others]
            grads.append([(a, 0, n * DH) for a in [res[0]] + moved])
        else:
            grads.append([(gather(res[0]), 0, n * DH)])
        carried, first = res[1], first + n
    own_pair = res[1]
    mark = marker(pieces[0]) if bit == 1 else None
    own_pair = pair_total(own_pair, arrived, mark)
    if pairwise:
        last = [(a, 0, kv) for a in [own_pair] + [swap(own_pair, k) for k in others]]
    else:
        last = [(gather(own_pair), 0, kv)]
    grads.append(last)
    cols.append(kv)
    part = input_part(pieces, weight)
    input_grad = input_gradient(part, own_pair, weight, scale)

    target = None
    ready = []
    first = 0
    for chunk, n, tag in zip(grads, cols, tags + "c"):
        updated, sent = update(rate, columns, chunk, weight, first, share, scale)
        ready.append((updated, partner(sent), first))
        if tag == "c" or not alone:
            target = average(target, ready, weight.shape[1])
            ready = []
        first += n
    return target[None], input_grad[None]


def per_device(tokens_in, qkv_weight, out_cotangent, step_index):
    levels = lax.axis_size("rep").bit_length() - 1

    def branch(bit):
        def run(*args):
            return step(*args, bit=bit)

        return run

    return lax.switch(
        step_index[0] % levels,
        [branch(bit) for bit in range(levels)],
        tokens_in[0],
        qkv_weight[0],
        out_cotangent[0],
        step_index,
    )


def solution(mesh):
    return jax.shard_map(
        per_device,
        mesh=mesh,
        in_specs=(P("rep", "seq", None), P("rep", None, None), P("rep", "seq", None), P()),
        out_specs=(P("rep", "seq", None), P("rep", "seq", None)),
        check_vma=False,
    )
```

profile of v0, /device:TPU:0, one launch (start us, length us, event | category | flops | bytes accessed | tf_op | source)
XLA Modules:
  0.0 49.3 jit_solution(5736408366033084200)
XLA Ops:
  1.3 47.8 %conditional.1 = (f32[1,384,1024]{2,1,0:T(8,128)}, bf16[1,128,1536]{2,1,0:T(8,128)(2,1)}) conditional(s32[]{:T(128)} %clamp.3, (bf16[1,128,1536]{2,1,0:T(8,128)(2,1)}, bf16[1,1536,1024]{2,1,0:T(8,128)(2,1)}, s32[1]{0:T(128)}, bf16[1,128,768]{2,1,0:T(8,128)(2,1)}) %tuple.22, (bf16[1,128,1536]{2,1,0:T(8,128)(2,1)}, ...), branch_computations={%region_0.1_spmd, %region_1.2_spmd, %region_2.3_spmd} | conditional | bytes 22414264 | solution.py:423
  1.3 1.7 %kv_project.3 = (bf16[128,256]{1,0:T(8,128)(2,1)S(1)}, bf16[128,1536]{1,0:T(8,128)(2,1)S(1)}) custom-call(bf16[128,1536]{1,0:T(8,128)(2,1)} %bitcast.46, bf16[1536,1024]{1,0:T(8,128)(2,1)} %bitcast.16), custom_call_target="tpu_custom_call" | custom-call | tf_op jit(solution)/shard_map/cond/branch_0_fun/kv_project/pallas_call | solution.py:75
  3.0 3.0 %collective-permute-start.3 = (bf16[128,256]{1,0:T(8,128)(2,1)S(1)}, bf16[128,256]{1,0:T(8,128)(2,1)S(1)}, u32[]{:S(2)}, u32[]{:S(2)}) collective-permute-start(bf16[128,256]{1,0:T(8,128)(2,1)S(1)} %get-tuple-element.38.refs_2_), channel_id=1, source_target_pairs={{0,1},{1,0},{2,3},{3,2},{4,5},{5,4},{6,7},{7,6},{8,9},{9,8},{10,11... | collective-permute-start | bytes 196616 | tf_op jit(solution)/shard_map/cond/branch_0_fun/ppermute | solution.py:334
  6.1 1.5 %collective-permute-start.4 = (bf16[128,256]{1,0:T(8,128)(2,1)S(1)}, bf16[128,256]{1,0:T(8,128)(2,1)S(1)}, u32[]{:S(2)}, u32[]{:S(2)}) collective-permute-start(bf16[128,256]{1,0:T(8,128)(2,1)S(1)} %get-tuple-element.38.refs_2_), channel_id=1, source_target_pairs={{0,2},{1,3},{2,0},{3,1},{4,6},{5,7},{6,4},{7,5},{8,10},{9,11},{10,... | collective-permute-start | bytes 196616 | tf_op jit(solution)/shard_map/cond/branch_0_fun/ppermute | solution.py:334
  7.6 0.5 %branch_0_fun.8 = (bf16[128,768]{1,0:T(8,128)(2,1)S(1)}, bf16[128,384]{1,0:T(8,128)(2,1)S(1)}, bf16[128,384]{1,0:T(8,128)(2,1)S(1)}, bf16[128,384]{1,0:T(8,128)(2,1)S(1)}, bf16[128,384]{1,0:T(8,128)(2,1)S(1)}) custom-call(bf16[128,1536]{1,0:T(8,128)(2,1)S(1)} %get-tuple-element.27.x_ref, bf16[1536,1024]{1,0:T(8,128)(2,1)S(1)} %bitcast.17), custom_call_target="tpu_custom_call" | custom-call | tf_op jit(solution)/shard_map/cond/branch_0_fun/pallas_call | solution.py:39
  8.1 2.0 %collective-permute-start = (bf16[128,384]{1,0:T(8,128)(2,1)S(1)}, bf16[128,384]{1,0:T(8,128)(2,1)S(1)}, u32[]{:S(2)}, u32[]{:S(2)}) collective-permute-start(bf16[128,384]{1,0:T(8,128)(2,1)S(1)} %get-tuple-element.31), channel_id=1, source_target_pairs={{0,1},{1,0},{2,3},{3,2},{4,5},{5,4},{6,7},{7,6},{8,9},{9,8},{10,11... | collective-permute-start | bytes 294920 | tf_op jit(solution)/shard_map/cond/branch_0_fun/ppermute | solution.py:334
  10.1 0.2 collective-permute-done.4.refs_4_
  10.3 2.6 %collective-permute-done.5.refs_5_ = bf16[128,256]{1,0:T(8,128)(2,1)S(1)} collective-permute-done((bf16[128,256]{1,0:T(8,128)(2,1)S(1)}, bf16[128,256]{1,0:T(8,128)(2,1)S(1)}, u32[]{:S(2)}, u32[]{:S(2)}) %collective-permute-start.5) | collective-permute-done | bytes 65568 | tf_op jit(solution)/shard_map/cond/branch_0_fun/ppermute | solution.py:334
  13.0 2.4 %branch_0_fun.10 = (bf16[128,768]{1,0:T(8,128)(2,1)S(1)}, f32[128,256]{1,0:T(8,128)S(1)}, bf16[128,256]{1,0:T(8,128)(2,1)S(1)}, bf16[128,256]{1,0:T(8,128)(2,1)S(1)}, bf16[128,256]{1,0:T(8,128)(2,1)S(1)}) custom-call(bf16[128,768]{1,0:T(8,128)(2,1)S(1)} %get-tuple-element.36.refs_0_, bf16[128,768]{1,0:T(8,128)(2,1)S(1)} %bitcast.37, ...), custom_call_target="tpu_custom_call" | custom-call | tf_op jit(solution)/shard_map/cond/branch_0_fun/pallas_call | solution.py:39
  15.3 1.0 %collective-permute-start.6 = (bf16[128,768]{1,0:T(8,128)(2,1)S(1)}, bf16[128,768]{1,0:T(8,128)(2,1)S(1)}, u32[]{:S(2)}, u32[]{:S(2)}) collective-permute-start(bf16[128,768]{1,0:T(8,128)(2,1)S(1)} %get-tuple-element.39.refs_0_), channel_id=1, source_target_pairs={{0,1},{1,0},{2,3},{3,2},{4,5},{5,4},{6,7},{7,6},{8,9},{9,8},{10,11... | collective-permute-start | bytes 589832 | tf_op jit(solution)/shard_map/cond/branch_0_fun/ppermute | solution.py:334
  16.3 2.6 %collective-permute-start.8 = (bf16[128,768]{1,0:T(8,128)(2,1)S(1)}, bf16[128,768]{1,0:T(8,128)(2,1)S(1)}, u32[]{:S(2)}, u32[]{:S(2)}) collective-permute-start(bf16[128,768]{1,0:T(8,128)(2,1)S(1)} %get-tuple-element.39.refs_0_), channel_id=1, source_target_pairs={{0,3},{1,2},{2,1},{3,0},{4,7},{5,6},{6,5},{7,4},{8,11},{9,10},{10,... | collective-permute-start | bytes 589832 | tf_op jit(solution)/shard_map/cond/branch_0_fun/ppermute | solution.py:334
  18.9 0.4 collective-permute-start.1
  19.3 2.0 %collective-permute-start.2 = (bf16[128,384]{1,0:T(8,128)(2,1)S(1)}, bf16[128,384]{1,0:T(8,128)(2,1)S(1)}, u32[]{:S(2)}, u32[]{:S(2)}) collective-permute-start(bf16[128,384]{1,0:T(8,128)(2,1)S(1)} %get-tuple-element.33), channel_id=1, source_target_pairs={{0,3},{1,2},{2,1},{3,0},{4,7},{5,6},{6,5},{7,4},{8,11},{9,10},{10,... | collective-permute-start | bytes 294920 | tf_op jit(solution)/shard_map/cond/branch_0_fun/ppermute | solution.py:334
  21.3 7.9 %collective-permute-done.1.refs_2_ = bf16[128,384]{1,0:T(8,128)(2,1)S(1)} collective-permute-done((bf16[128,384]{1,0:T(8,128)(2,1)S(1)}, bf16[128,384]{1,0:T(8,128)(2,1)S(1)}, u32[]{:S(2)}, u32[]{:S(2)}) %collective-permute-start.1) | collective-permute-done | bytes 98336 | tf_op jit(solution)/shard_map/cond/branch_0_fun/ppermute | solution.py:334
  29.2 0.8 %branch_0_fun.9 = (bf16[384,512]{1,0:T(8,128)(2,1)S(1)}, f32[8,128]{1,0:T(8,128)S(1)}) custom-call(s32[1]{0:T(128)} %get-tuple-element.24.s_ref, bf16[128,384]{1,0:T(8,128)(2,1)S(1)} %get-tuple-element.30.refs_0_, bf16[128,384]{1,0:T(8,128)(2,1)S(1)} %collective-permute-done.refs_1_, bf16[128,384]{1,0:T(8,128)(2,1)S(1)} %collective-permute-done.1.refs_2_, ...), custom_call_target="tpu_custom_call" | custom-call | tf_op jit(solution)/shard_map/cond/branch_0_fun/pallas_call | solution.py:39
  30.1 0.5 %branch_0_fun.11 = (f32[384,768]{1,0:T(8,128)S(1)}, bf16[384,768]{1,0:T(8,128)(2,1)S(1)}) custom-call(f32[8,128]{1,0:T(8,128)S(1)} %get-tuple-element.34.rate_ref, bf16[384,512]{1,0:T(8,128)(2,1)S(1)} %get-tuple-element.35.x_ref, bf16[128,768]{1,0:T(8,128)(2,1)S(1)} %get-tuple-element.39.refs_0_, bf16[128,768]{1,0:T(8,128)(2,1)S(1)} %collective-permute-done.6.refs_1_, ...), custom_call_target="tpu_custom_call" | custom-call | tf_op jit(solution)/shard_map/cond/branch_0_fun/pallas_call | solution.py:39
  30.6 1.2 %collective-permute-start.10 = (bf16[128,256]{1,0:T(8,128)(2,1)S(1)}, bf16[128,256]{1,0:T(8,128)(2,1)S(1)}, u32[]{:S(2)}, u32[]{:S(2)}) collective-permute-start(bf16[128,256]{1,0:T(8,128)(2,1)S(1)} %get-tuple-element.43), channel_id=1, source_target_pairs={{0,1},{1,0},{2,3},{3,2},{4,5},{5,4},{6,7},{7,6},{8,9},{9,8},{10,11... | collective-permute-start | bytes 196616 | tf_op jit(solution)/shard_map/cond/branch_0_fun/ppermute | solution.py:334
  31.8 0.6 %collective-permute-start.11 = (bf16[128,256]{1,0:T(8,128)(2,1)S(1)}, bf16[128,256]{1,0:T(8,128)(2,1)S(1)}, u32[]{:S(2)}, u32[]{:S(2)}) collective-permute-start(bf16[128,256]{1,0:T(8,128)(2,1)S(1)} %get-tuple-element.44), channel_id=1, source_target_pairs={{0,2},{1,3},{2,0},{3,1},{4,6},{5,7},{6,4},{7,5},{8,10},{9,11},{10,... | collective-permute-start | bytes 196616 | tf_op jit(solution)/shard_map/cond/branch_0_fun/ppermute | solution.py:334
  32.3 1.8 %collective-permute-start.12 = (bf16[128,256]{1,0:T(8,128)(2,1)S(1)}, bf16[128,256]{1,0:T(8,128)(2,1)S(1)}, u32[]{:S(2)}, u32[]{:S(2)}) collective-permute-start(bf16[128,256]{1,0:T(8,128)(2,1)S(1)} %get-tuple-element.45), channel_id=1, source_target_pairs={{0,3},{1,2},{2,1},{3,0},{4,7},{5,6},{6,5},{7,4},{8,11},{9,10},{10,... | collective-permute-start | bytes 196616 | tf_op jit(solution)/shard_map/cond/branch_0_fun/ppermute | solution.py:334
  34.2 0.9 %collective-permute-done.10.refs_1_ = bf16[128,256]{1,0:T(8,128)(2,1)S(1)} collective-permute-done((bf16[128,256]{1,0:T(8,128)(2,1)S(1)}, bf16[128,256]{1,0:T(8,128)(2,1)S(1)}, u32[]{:S(2)}, u32[]{:S(2)}) %collective-permute-start.10) | collective-permute-done | bytes 65568 | tf_op jit(solution)/shard_map/cond/branch_0_fun/ppermute | solution.py:334
  35.1 1.6 %collective-permute-done.11.refs_2_ = bf16[128,256]{1,0:T(8,128)(2,1)S(1)} collective-permute-done((bf16[128,256]{1,0:T(8,128)(2,1)S(1)}, bf16[128,256]{1,0:T(8,128)(2,1)S(1)}, u32[]{:S(2)}, u32[]{:S(2)}) %collective-permute-start.11) | collective-permute-done | bytes 65568 | tf_op jit(solution)/shard_map/cond/branch_0_fun/ppermute | solution.py:334
  36.8 0.7 %collective-permute-done.12.refs_3_ = bf16[128,256]{1,0:T(8,128)(2,1)S(1)} collective-permute-done((bf16[128,256]{1,0:T(8,128)(2,1)S(1)}, bf16[128,256]{1,0:T(8,128)(2,1)S(1)}, u32[]{:S(2)}, u32[]{:S(2)}) %collective-permute-start.12) | collective-permute-done | bytes 65568 | tf_op jit(solution)/shard_map/cond/branch_0_fun/ppermute | solution.py:334
  37.5 1.1 %collective-permute-start.13 = (bf16[128,256]{1,0:T(8,128)(2,1)S(1)}, bf16[128,256]{1,0:T(8,128)(2,1)S(1)}, u32[]{:S(2)}, u32[]{:S(2)}) collective-permute-start(bf16[128,256]{1,0:T(8,128)(2,1)S(1)} %branch_0_fun.12.refs_0_.g_ref), channel_id=1, source_target_pairs={{0,1},{1,0},{2,3},{3,2},{4,5},{5,4},{6,7},{7,6},{8,9},{9,8},{10,11... | collective-permute-start | bytes 196616 | tf_op jit(solution)/shard_map/cond/branch_0_fun/ppermute | solution.py:334
  38.6 1.4 %collective-permute-start.14 = (bf16[128,256]{1,0:T(8,128)(2,1)S(1)}, bf16[128,256]{1,0:T(8,128)(2,1)S(1)}, u32[]{:S(2)}, u32[]{:S(2)}) collective-permute-start(bf16[128,256]{1,0:T(8,128)(2,1)S(1)} %branch_0_fun.12.refs_0_.g_ref), channel_id=1, source_target_pairs={{0,2},{1,3},{2,0},{3,1},{4,6},{5,7},{6,4},{7,5},{8,10},{9,11},{10,... | collective-permute-start | bytes 196616 | tf_op jit(solution)/shard_map/cond/branch_0_fun/ppermute | solution.py:334
  40.0 1.1 %collective-permute-start.15 = (bf16[128,256]{1,0:T(8,128)(2,1)S(1)}, bf16[128,256]{1,0:T(8,128)(2,1)S(1)}, u32[]{:S(2)}, u32[]{:S(2)}) collective-permute-start(bf16[128,256]{1,0:T(8,128)(2,1)S(1)} %branch_0_fun.12.refs_0_.g_ref), channel_id=1, source_target_pairs={{0,3},{1,2},{2,1},{3,0},{4,7},{5,6},{6,5},{7,4},{8,11},{9,10},{10,... | collective-permute-start | bytes 196616 | tf_op jit(solution)/shard_map/cond/branch_0_fun/ppermute | solution.py:334
  41.1 1.2 %collective-permute-done.13.refs_1_ = bf16[128,256]{1,0:T(8,128)(2,1)S(1)} collective-permute-done((bf16[128,256]{1,0:T(8,128)(2,1)S(1)}, bf16[128,256]{1,0:T(8,128)(2,1)S(1)}, u32[]{:S(2)}, u32[]{:S(2)}) %collective-permute-start.13) | collective-permute-done | bytes 65568 | tf_op jit(solution)/shard_map/cond/branch_0_fun/ppermute | solution.py:334
  42.3 0.8 %collective-permute-done.14.refs_2_ = bf16[128,256]{1,0:T(8,128)(2,1)S(1)} collective-permute-done((bf16[128,256]{1,0:T(8,128)(2,1)S(1)}, bf16[128,256]{1,0:T(8,128)(2,1)S(1)}, u32[]{:S(2)}, u32[]{:S(2)}) %collective-permute-start.14) | collective-permute-done | bytes 65568 | tf_op jit(solution)/shard_map/cond/branch_0_fun/ppermute | solution.py:334
  43.1 2.1 %collective-permute-done.15.refs_3_ = bf16[128,256]{1,0:T(8,128)(2,1)S(1)} collective-permute-done((bf16[128,256]{1,0:T(8,128)(2,1)S(1)}, bf16[128,256]{1,0:T(8,128)(2,1)S(1)}, u32[]{:S(2)}, u32[]{:S(2)}) %collective-permute-start.15) | collective-permute-done | bytes 65568 | tf_op jit(solution)/shard_map/cond/branch_0_fun/ppermute | solution.py:334
  45.2 0.3 branch_0_fun.13
  45.5 0.9 %branch_0_fun.15.part_ref = f32[128,1536]{1,0:T(8,128)S(1)} custom-call(bf16[128,768]{1,0:T(8,128)(2,1)S(1)} %get-tuple-element.39.refs_0_, bf16[1536,1024]{1,0:T(8,128)(2,1)S(1)} %bitcast.20), custom_call_target="tpu_custom_call" | custom-call | tf_op jit(solution)/shard_map/cond/branch_0_fun/pallas_call | solution.py:39
  46.4 1.2 %input_gradient.3 = bf16[128,1536]{1,0:T(8,128)(2,1)} custom-call(f32[128,1536]{1,0:T(8,128)S(1)} %branch_0_fun.15.part_ref, bf16[128,256]{1,0:T(8,128)(2,1)S(1)} %branch_0_fun.12.refs_0_.g_ref, bf16[1536,1024]{1,0:T(8,128)(2,1)S(1)} %bitcast.21), custom_call_target="tpu_custom_call" | custom-call | tf_op jit(solution)/shard_map/cond/branch_0_fun/input_gradient/pallas_call | solution.py:305
  47.6 1.2 %branch_0_fun.14 = f32[384,1024]{1,0:T(8,128)} custom-call(f32[384,768]{1,0:T(8,128)S(1)} %get-tuple-element.40.refs_0_, bf16[384,768]{1,0:T(8,128)(2,1)S(1)} %collective-permute-done.9.refs_1_, f32[384,256]{1,0:T(8,128)S(1)} %get-tuple-element.46.refs_2_, bf16[384,256]{1,0:T(8,128)(2,1)S(1)} %collective-permute-done.16.refs_3_), custom_call_target="tpu_custom_call" | custom-call | tf_op jit(solution)/shard_map/cond/branch_0_fun/pallas_call | solution.py:247
  (17 shorter events, 0.2 us)
Async XLA Ops:
  1.3 6.3 %copy-start = (bf16[1,1536,1024]{2,1,0:T(8,128)(2,1)S(1)}, bf16[1,1536,1024]{2,1,0:T(8,128)(2,1)}, u32[]{:S(2)}) copy-start(bf16[1,1536,1024]{2,1,0:T(8,128)(2,1)} %get-tuple-element.133) | copy-start | bytes 9437188 | tf_op jit(solution)/shard_map/cond
  3.0 7.1 %collective-permute-start.3 = (bf16[128,256]{1,0:T(8,128)(2,1)S(1)}, bf16[128,256]{1,0:T(8,128)(2,1)S(1)}, u32[]{:S(2)}, u32[]{:S(2)}) collective-permute-start(bf16[128,256]{1,0:T(8,128)(2,1)S(1)} %get-tuple-element.38.refs_2_), channel_id=1, source_target_pairs={{0,1},{1,0},{2,3},{3,2},{4,5},{5,4},{6,7},{7,6},{8,9},{9,8},{10,11... | collective-permute-start | bytes 196616 | tf_op jit(solution)/shard_map/cond/branch_0_fun/ppermute | solution.py:334
  6.1 4.3 %collective-permute-start.4 = (bf16[128,256]{1,0:T(8,128)(2,1)S(1)}, bf16[128,256]{1,0:T(8,128)(2,1)S(1)}, u32[]{:S(2)}, u32[]{:S(2)}) collective-permute-start(bf16[128,256]{1,0:T(8,128)(2,1)S(1)} %get-tuple-element.38.refs_2_), channel_id=1, source_target_pairs={{0,2},{1,3},{2,0},{3,1},{4,6},{5,7},{6,4},{7,5},{8,10},{9,11},{10,... | collective-permute-start | bytes 196616 | tf_op jit(solution)/shard_map/cond/branch_0_fun/ppermute | solution.py:334
  7.6 5.4 %collective-permute-start.5 = (bf16[128,256]{1,0:T(8,128)(2,1)S(1)}, bf16[128,256]{1,0:T(8,128)(2,1)S(1)}, u32[]{:S(2)}, u32[]{:S(2)}) collective-permute-start(bf16[128,256]{1,0:T(8,128)(2,1)S(1)} %get-tuple-element.38.refs_2_), channel_id=1, source_target_pairs={{0,3},{1,2},{2,1},{3,0},{4,7},{5,6},{6,5},{7,4},{8,11},{9,10},{10,... | collective-permute-start | bytes 196616 | tf_op jit(solution)/shard_map/cond/branch_0_fun/ppermute | solution.py:334
  7.6 5.4 %copy-start.3 = (bf16[1,128,768]{2,1,0:T(8,128)(2,1)S(1)}, bf16[1,128,768]{2,1,0:T(8,128)(2,1)}, u32[]{:S(2)}) copy-start(bf16[1,128,768]{2,1,0:T(8,128)(2,1)} %get-tuple-element.136) | copy-start | bytes 589828 | tf_op jit(solution)/shard_map/cond
  8.1 11.1 %collective-permute-start = (bf16[128,384]{1,0:T(8,128)(2,1)S(1)}, bf16[128,384]{1,0:T(8,128)(2,1)S(1)}, u32[]{:S(2)}, u32[]{:S(2)}) collective-permute-start(bf16[128,384]{1,0:T(8,128)(2,1)S(1)} %get-tuple-element.31), channel_id=1, source_target_pairs={{0,1},{1,0},{2,3},{3,2},{4,5},{5,4},{6,7},{7,6},{8,9},{9,8},{10,11... | collective-permute-start | bytes 294920 | tf_op jit(solution)/shard_map/cond/branch_0_fun/ppermute | solution.py:334
  15.3 14.7 %collective-permute-start.6 = (bf16[128,768]{1,0:T(8,128)(2,1)S(1)}, bf16[128,768]{1,0:T(8,128)(2,1)S(1)}, u32[]{:S(2)}, u32[]{:S(2)}) collective-permute-start(bf16[128,768]{1,0:T(8,128)(2,1)S(1)} %get-tuple-element.39.refs_0_), channel_id=1, source_target_pairs={{0,1},{1,0},{2,3},{3,2},{4,5},{5,4},{6,7},{7,6},{8,9},{9,8},{10,11... | collective-permute-start | bytes 589832 | tf_op jit(solution)/shard_map/cond/branch_0_fun/ppermute | solution.py:334
  16.3 13.7 %collective-permute-start.7 = (bf16[128,768]{1,0:T(8,128)(2,1)S(1)}, bf16[128,768]{1,0:T(8,128)(2,1)S(1)}, u32[]{:S(2)}, u32[]{:S(2)}) collective-permute-start(bf16[128,768]{1,0:T(8,128)(2,1)S(1)} %get-tuple-element.39.refs_0_), channel_id=1, source_target_pairs={{0,2},{1,3},{2,0},{3,1},{4,6},{5,7},{6,4},{7,5},{8,10},{9,11},{10,... | collective-permute-start | bytes 589832 | tf_op jit(solution)/shard_map/cond/branch_0_fun/ppermute | solution.py:334
  16.3 13.7 %collective-permute-start.8 = (bf16[128,768]{1,0:T(8,128)(2,1)S(1)}, bf16[128,768]{1,0:T(8,128)(2,1)S(1)}, u32[]{:S(2)}, u32[]{:S(2)}) collective-permute-start(bf16[128,768]{1,0:T(8,128)(2,1)S(1)} %get-tuple-element.39.refs_0_), channel_id=1, source_target_pairs={{0,3},{1,2},{2,1},{3,0},{4,7},{5,6},{6,5},{7,4},{8,11},{9,10},{10,... | collective-permute-start | bytes 589832 | tf_op jit(solution)/shard_map/cond/branch_0_fun/ppermute | solution.py:334
  18.9 10.3 %collective-permute-start.1 = (bf16[128,384]{1,0:T(8,128)(2,1)S(1)}, bf16[128,384]{1,0:T(8,128)(2,1)S(1)}, u32[]{:S(2)}, u32[]{:S(2)}) collective-permute-start(bf16[128,384]{1,0:T(8,128)(2,1)S(1)} %get-tuple-element.32), channel_id=1, source_target_pairs={{0,2},{1,3},{2,0},{3,1},{4,6},{5,7},{6,4},{7,5},{8,10},{9,11},{10,... | collective-permute-start | bytes 294920 | tf_op jit(solution)/shard_map/cond/branch_0_fun/ppermute | solution.py:334
  19.3 10.0 %collective-permute-start.2 = (bf16[128,384]{1,0:T(8,128)(2,1)S(1)}, bf16[128,384]{1,0:T(8,128)(2,1)S(1)}, u32[]{:S(2)}, u32[]{:S(2)}) collective-permute-start(bf16[128,384]{1,0:T(8,128)(2,1)S(1)} %get-tuple-element.33), channel_id=1, source_target_pairs={{0,3},{1,2},{2,1},{3,0},{4,7},{5,6},{6,5},{7,4},{8,11},{9,10},{10,... | collective-permute-start | bytes 294920 | tf_op jit(solution)/shard_map/cond/branch_0_fun/ppermute | solution.py:334
  30.6 17.1 %collective-permute-start.9 = (bf16[384,768]{1,0:T(8,128)(2,1)S(1)}, bf16[384,768]{1,0:T(8,128)(2,1)S(1)}, u32[]{:S(2)}, u32[]{:S(2)}) collective-permute-start(bf16[384,768]{1,0:T(8,128)(2,1)S(1)} %get-tuple-element.41), channel_id=1, source_target_pairs={{0,4},{4,0},{8,12},{12,8},{16,20},{20,16},{24,28},{28,24},{1,5},{5... | collective-permute-start | bytes 1769480 | tf_op jit(solution)/shard_map/cond/branch_0_fun/ppermute | solution.py:344
  30.6 4.5 %collective-permute-start.10 = (bf16[128,256]{1,0:T(8,128)(2,1)S(1)}, bf16[128,256]{1,0:T(8,128)(2,1)S(1)}, u32[]{:S(2)}, u32[]{:S(2)}) collective-permute-start(bf16[128,256]{1,0:T(8,128)(2,1)S(1)} %get-tuple-element.43), channel_id=1, source_target_pairs={{0,1},{1,0},{2,3},{3,2},{4,5},{5,4},{6,7},{7,6},{8,9},{9,8},{10,11... | collective-permute-start | bytes 196616 | tf_op jit(solution)/shard_map/cond/branch_0_fun/ppermute | solution.py:334
  31.8 5.0 %collective-permute-start.11 = (bf16[128,256]{1,0:T(8,128)(2,1)S(1)}, bf16[128,256]{1,0:T(8,128)(2,1)S(1)}, u32[]{:S(2)}, u32[]{:S(2)}) collective-permute-start(bf16[128,256]{1,0:T(8,128)(2,1)S(1)} %get-tuple-element.44), channel_id=1, source_target_pairs={{0,2},{1,3},{2,0},{3,1},{4,6},{5,7},{6,4},{7,5},{8,10},{9,11},{10,... | collective-permute-start | bytes 196616 | tf_op jit(solution)/shard_map/cond/branch_0_fun/ppermute | solution.py:334
  32.3 5.2 %collective-permute-start.12 = (bf16[128,256]{1,0:T(8,128)(2,1)S(1)}, bf16[128,256]{1,0:T(8,128)(2,1)S(1)}, u32[]{:S(2)}, u32[]{:S(2)}) collective-permute-start(bf16[128,256]{1,0:T(8,128)(2,1)S(1)} %get-tuple-element.45), channel_id=1, source_target_pairs={{0,3},{1,2},{2,1},{3,0},{4,7},{5,6},{6,5},{7,4},{8,11},{9,10},{10,... | collective-permute-start | bytes 196616 | tf_op jit(solution)/shard_map/cond/branch_0_fun/ppermute | solution.py:334
  37.5 4.8 %collective-permute-start.13 = (bf16[128,256]{1,0:T(8,128)(2,1)S(1)}, bf16[128,256]{1,0:T(8,128)(2,1)S(1)}, u32[]{:S(2)}, u32[]{:S(2)}) collective-permute-start(bf16[128,256]{1,0:T(8,128)(2,1)S(1)} %branch_0_fun.12.refs_0_.g_ref), channel_id=1, source_target_pairs={{0,1},{1,0},{2,3},{3,2},{4,5},{5,4},{6,7},{7,6},{8,9},{9,8},{10,11... | collective-permute-start | bytes 196616 | tf_op jit(solution)/shard_map/cond/branch_0_fun/ppermute | solution.py:334
  38.6 4.5 %collective-permute-start.14 = (bf16[128,256]{1,0:T(8,128)(2,1)S(1)}, bf16[128,256]{1,0:T(8,128)(2,1)S(1)}, u32[]{:S(2)}, u32[]{:S(2)}) collective-permute-start(bf16[128,256]{1,0:T(8,128)(2,1)S(1)} %branch_0_fun.12.refs_0_.g_ref), channel_id=1, source_target_pairs={{0,2},{1,3},{2,0},{3,1},{4,6},{5,7},{6,4},{7,5},{8,10},{9,11},{10,... | collective-permute-start | bytes 196616 | tf_op jit(solution)/shard_map/cond/branch_0_fun/ppermute | solution.py:334
  40.0 5.2 %collective-permute-start.15 = (bf16[128,256]{1,0:T(8,128)(2,1)S(1)}, bf16[128,256]{1,0:T(8,128)(2,1)S(1)}, u32[]{:S(2)}, u32[]{:S(2)}) collective-permute-start(bf16[128,256]{1,0:T(8,128)(2,1)S(1)} %branch_0_fun.12.refs_0_.g_ref), channel_id=1, source_target_pairs={{0,3},{1,2},{2,1},{3,0},{4,7},{5,6},{6,5},{7,4},{8,11},{9,10},{10,... | collective-permute-start | bytes 196616 | tf_op jit(solution)/shard_map/cond/branch_0_fun/ppermute | solution.py:334
  45.5 2.1 %collective-permute-start.16 = (bf16[384,256]{1,0:T(8,128)(2,1)S(1)}, bf16[384,256]{1,0:T(8,128)(2,1)S(1)}, u32[]{:S(2)}, u32[]{:S(2)}) collective-permute-start(bf16[384,256]{1,0:T(8,128)(2,1)S(1)} %get-tuple-element.47), channel_id=1, source_target_pairs={{0,4},{4,0},{8,12},{12,8},{16,20},{20,16},{24,28},{28,24},{1,5},{5... | collective-permute-start | bytes 589832 | tf_op jit(solution)/shard_map/cond/branch_0_fun/ppermute | solution.py:344
where the time goes:
time: 49.4 us; the launch traced here: 49.3 us
  starting transfers between devices  19.8 us (40%)
  waiting for transfers between devices  18.2 us (37%)
  Pallas kernels  9.49 us (19%)
  between operations  1.47 us (3%)
    ppermute x15, starting transfers between devices, swap(): return lax.ppermute(array, 'seq', xor_pairs(parts, key))  19.6 us
    ppermute x15, waiting for transfers between devices, swap(): return lax.ppermute(array, 'seq', xor_pairs(parts, key))  18.2 us
    pallas_call x7, Pallas kernels, local_call(): pl.pallas_call(body, out_shape=[VMEM(s, d) for s, d in shapes], in_specs=...  5.4 us
    pallas_call x1, Pallas kernels, kv_project(): pl.pallas_call(body, out_shape=[VMEM((rows, cols), BF16), VMEM((rows, wid...  1.7 us
    pallas_call x1, Pallas kernels, average(): pl.pallas_call(body, out_shape=HBM((share, width), F32), in_specs=specs,...  1.24 us
    pallas_call x1, Pallas kernels, input_gradient(): pl.pallas_call(body, out_shape=HBM((rows, width), BF16), in_specs=[pl.Blo...  1.15 us
  transfers between devices with their start and end apart: 17, of which 9 were waited for; matrix products, arithmetic and copies ran while one was open for 0% of the time, Pallas kernels for 12%

commit v1 on v0

--- a/solution.py
+++ b/solution.py
@@ -17,6 +17,7 @@
 SMEM = pltpu.MemorySpace.SMEM
 HBM = pltpu.MemorySpace.HBM
 GRANT = 16 << 20
+ORDER = {0: (2, 3, 1), 1: (1, 2, 3), 2: (3, 1, 2)}
 SPLIT = {0: (6,), 1: (4, 2), 2: (3, 1, 2)}
 
 
@@ -101,7 +102,7 @@
     count = len(blocks)
     cols = heads * DH
     kv = 2 * DH
-    group = 2
+    group = 6
     scale = DH ** (-0.5)
     factor = scale * LOG2E
     packed = packed and last
@@ -323,7 +324,7 @@
     share = width // parts
     hops = min(-(-(WINDOW + rows - 1) // rows) - 1, parts - 1)
     pairwise = hops == parts - 1 and parts in (2, 4) and share % 128 == 0
-    others = range(1, parts)
+    others = [k for k in ORDER[min(bit, 2)] if k < parts] if parts <= 4 else range(1, parts)
     near = range(1, hops + 1)
 
     def place_of(hop):

time: 49.4 us -> 48.6 us (0.984)
  Pallas kernels: 9.49 us -> 8.97 us
    pallas_call x7, Pallas kernels: 5.4 us -> 4.88 us  [local_call(): pl.pallas_call(body, out_shape=[VMEM(s, d) for s, d in shapes], in_specs=...]
  transfers between devices with their start and end apart: 17 -> 17, of which waited for: 9 -> 10; matrix products, arithmetic and copies ran while one was open for 0% -> 0% of each run, Pallas kernels for 12% -> 11%
where the time goes in v1:
time: 48.6 us; the launch traced here: 48.4 us
  starting transfers between devices  19.5 us (40%)
  waiting for transfers between devices  18.1 us (37%)
  Pallas kernels  8.97 us (18%)
  between operations  1.47 us (3%)
    ppermute x15, starting transfers between devices, swap(): return lax.ppermute(array, 'seq', xor_pairs(parts, key))  19.3 us
    ppermute x15, waiting for transfers between devices, swap(): return lax.ppermute(array, 'seq', xor_pairs(parts, key))  18.1 us
    pallas_call x7, Pallas kernels, local_call(): pl.pallas_call(body, out_shape=[VMEM(s, d) for s, d in shapes], in_specs=...  4.88 us
    pallas_call x1, Pallas kernels, kv_project(): pl.pallas_call(body, out_shape=[VMEM((rows, cols), BF16), VMEM((rows, wid...  1.7 us
    pallas_call x1, Pallas kernels, average(): pl.pallas_call(body, out_shape=HBM((share, width), F32), in_specs=specs,...  1.24 us
    pallas_call x1, Pallas kernels, input_gradient(): pl.pallas_call(body, out_shape=HBM((rows, width), BF16), in_specs=[pl.Blo...  1.15 us
  transfers between devices with their start and end apart: 17, of which 10 were waited for; matrix products, arithmetic and copies ran while one was open for 0% of the time, Pallas kernels for 11%

profile of v1, /device:TPU:0, one launch (start us, length us, event | category | flops | bytes accessed | tf_op | source)
XLA Modules:
  0.0 48.4 jit_solution(127684183040158283)
XLA Ops:
  1.3 47.0 %conditional.1 = (f32[1,384,1024]{2,1,0:T(8,128)}, bf16[1,128,1536]{2,1,0:T(8,128)(2,1)}) conditional(s32[]{:T(128)} %clamp.3, (bf16[1,128,1536]{2,1,0:T(8,128)(2,1)}, bf16[1,1536,1024]{2,1,0:T(8,128)(2,1)}, s32[1]{0:T(128)}, bf16[1,128,768]{2,1,0:T(8,128)(2,1)}) %tuple.22, (bf16[1,128,1536]{2,1,0:T(8,128)(2,1)}, ...), branch_computations={%region_0.1_spmd, %region_1.2_spmd, %region_2.3_spmd} | conditional | bytes 22414264 | solution.py:424
  1.3 1.7 %kv_project.3 = (bf16[128,256]{1,0:T(8,128)(2,1)S(1)}, bf16[128,1536]{1,0:T(8,128)(2,1)S(1)}) custom-call(bf16[128,1536]{1,0:T(8,128)(2,1)} %bitcast.46, bf16[1536,1024]{1,0:T(8,128)(2,1)} %bitcast.16), custom_call_target="tpu_custom_call" | custom-call | tf_op jit(solution)/shard_map/cond/branch_0_fun/kv_project/pallas_call | solution.py:76
  3.0 3.0 %collective-permute-start.3 = (bf16[128,256]{1,0:T(8,128)(2,1)S(1)}, bf16[128,256]{1,0:T(8,128)(2,1)S(1)}, u32[]{:S(2)}, u32[]{:S(2)}) collective-permute-start(bf16[128,256]{1,0:T(8,128)(2,1)S(1)} %get-tuple-element.38.refs_2_), channel_id=1, source_target_pairs={{0,1},{1,0},{2,3},{3,2},{4,5},{5,4},{6,7},{7,6},{8,9},{9,8},{10,11... | collective-permute-start | bytes 196616 | tf_op jit(solution)/shard_map/cond/branch_0_fun/ppermute | solution.py:335
  6.1 1.5 %collective-permute-start.4 = (bf16[128,256]{1,0:T(8,128)(2,1)S(1)}, bf16[128,256]{1,0:T(8,128)(2,1)S(1)}, u32[]{:S(2)}, u32[]{:S(2)}) collective-permute-start(bf16[128,256]{1,0:T(8,128)(2,1)S(1)} %get-tuple-element.38.refs_2_), channel_id=1, source_target_pairs={{0,2},{1,3},{2,0},{3,1},{4,6},{5,7},{6,4},{7,5},{8,10},{9,11},{10,... | collective-permute-start | bytes 196616 | tf_op jit(solution)/shard_map/cond/branch_0_fun/ppermute | solution.py:335
  7.6 0.5 %branch_0_fun.8 = (bf16[128,768]{1,0:T(8,128)(2,1)S(1)}, bf16[128,384]{1,0:T(8,128)(2,1)S(1)}, bf16[128,384]{1,0:T(8,128)(2,1)S(1)}, bf16[128,384]{1,0:T(8,128)(2,1)S(1)}, bf16[128,384]{1,0:T(8,128)(2,1)S(1)}) custom-call(bf16[128,1536]{1,0:T(8,128)(2,1)S(1)} %get-tuple-element.27.x_ref, bf16[1536,1024]{1,0:T(8,128)(2,1)S(1)} %bitcast.17), custom_call_target="tpu_custom_call" | custom-call | tf_op jit(solution)/shard_map/cond/branch_0_fun/pallas_call | solution.py:40
  8.1 2.0 %collective-permute-start = (bf16[128,384]{1,0:T(8,128)(2,1)S(1)}, bf16[128,384]{1,0:T(8,128)(2,1)S(1)}, u32[]{:S(2)}, u32[]{:S(2)}) collective-permute-start(bf16[128,384]{1,0:T(8,128)(2,1)S(1)} %get-tuple-element.31), channel_id=1, source_target_pairs={{0,2},{1,3},{2,0},{3,1},{4,6},{5,7},{6,4},{7,5},{8,10},{9,11},{10,... | collective-permute-start | bytes 294920 | tf_op jit(solution)/shard_map/cond/branch_0_fun/ppermute | solution.py:335
  10.2 1.1 %collective-permute-done.4.refs_4_ = bf16[128,256]{1,0:T(8,128)(2,1)S(1)} collective-permute-done((bf16[128,256]{1,0:T(8,128)(2,1)S(1)}, bf16[128,256]{1,0:T(8,128)(2,1)S(1)}, u32[]{:S(2)}, u32[]{:S(2)}) %collective-permute-start.4) | collective-permute-done | bytes 65568 | tf_op jit(solution)/shard_map/cond/branch_0_fun/ppermute | solution.py:335
  11.3 1.6 %collective-permute-done.5.refs_5_ = bf16[128,256]{1,0:T(8,128)(2,1)S(1)} collective-permute-done((bf16[128,256]{1,0:T(8,128)(2,1)S(1)}, bf16[128,256]{1,0:T(8,128)(2,1)S(1)}, u32[]{:S(2)}, u32[]{:S(2)}) %collective-permute-start.5) | collective-permute-done | bytes 65568 | tf_op jit(solution)/shard_map/cond/branch_0_fun/ppermute | solution.py:335
  12.8 1.9 %branch_0_fun.10 = (bf16[128,768]{1,0:T(8,128)(2,1)S(1)}, f32[128,256]{1,0:T(8,128)S(1)}, bf16[128,256]{1,0:T(8,128)(2,1)S(1)}, bf16[128,256]{1,0:T(8,128)(2,1)S(1)}, bf16[128,256]{1,0:T(8,128)(2,1)S(1)}) custom-call(bf16[128,768]{1,0:T(8,128)(2,1)S(1)} %get-tuple-element.36.refs_0_, bf16[128,768]{1,0:T(8,128)(2,1)S(1)} %bitcast.37, ...), custom_call_target="tpu_custom_call" | custom-call | tf_op jit(solution)/shard_map/cond/branch_0_fun/pallas_call | solution.py:40
  14.7 0.7 %collective-permute-start.6 = (bf16[128,768]{1,0:T(8,128)(2,1)S(1)}, bf16[128,768]{1,0:T(8,128)(2,1)S(1)}, u32[]{:S(2)}, u32[]{:S(2)}) collective-permute-start(bf16[128,768]{1,0:T(8,128)(2,1)S(1)} %get-tuple-element.39.refs_0_), channel_id=1, source_target_pairs={{0,2},{1,3},{2,0},{3,1},{4,6},{5,7},{6,4},{7,5},{8,10},{9,11},{10,... | collective-permute-start | bytes 589832 | tf_op jit(solution)/shard_map/cond/branch_0_fun/ppermute | solution.py:335
  15.4 1.4 %collective-permute-start.7 = (bf16[128,768]{1,0:T(8,128)(2,1)S(1)}, bf16[128,768]{1,0:T(8,128)(2,1)S(1)}, u32[]{:S(2)}, u32[]{:S(2)}) collective-permute-start(bf16[128,768]{1,0:T(8,128)(2,1)S(1)} %get-tuple-element.39.refs_0_), channel_id=1, source_target_pairs={{0,3},{1,2},{2,1},{3,0},{4,7},{5,6},{6,5},{7,4},{8,11},{9,10},{10,... | collective-permute-start | bytes 589832 | tf_op jit(solution)/shard_map/cond/branch_0_fun/ppermute | solution.py:335
  16.8 1.5 %collective-permute-start.8 = (bf16[128,768]{1,0:T(8,128)(2,1)S(1)}, bf16[128,768]{1,0:T(8,128)(2,1)S(1)}, u32[]{:S(2)}, u32[]{:S(2)}) collective-permute-start(bf16[128,768]{1,0:T(8,128)(2,1)S(1)} %get-tuple-element.39.refs_0_), channel_id=1, source_target_pairs={{0,1},{1,0},{2,3},{3,2},{4,5},{5,4},{6,7},{7,6},{8,9},{9,8},{10,11... | collective-permute-start | bytes 589832 | tf_op jit(solution)/shard_map/cond/branch_0_fun/ppermute | solution.py:335
  18.3 0.4 collective-permute-start.1
  18.6 1.7 %collective-permute-start.2 = (bf16[128,384]{1,0:T(8,128)(2,1)S(1)}, bf16[128,384]{1,0:T(8,128)(2,1)S(1)}, u32[]{:S(2)}, u32[]{:S(2)}) collective-permute-start(bf16[128,384]{1,0:T(8,128)(2,1)S(1)} %get-tuple-element.33), channel_id=1, source_target_pairs={{0,1},{1,0},{2,3},{3,2},{4,5},{5,4},{6,7},{7,6},{8,9},{9,8},{10,11... | collective-permute-start | bytes 294920 | tf_op jit(solution)/shard_map/cond/branch_0_fun/ppermute | solution.py:335
  20.3 7.9 %collective-permute-done.1.refs_2_ = bf16[128,384]{1,0:T(8,128)(2,1)S(1)} collective-permute-done((bf16[128,384]{1,0:T(8,128)(2,1)S(1)}, bf16[128,384]{1,0:T(8,128)(2,1)S(1)}, u32[]{:S(2)}, u32[]{:S(2)}) %collective-permute-start.1) | collective-permute-done | bytes 98336 | tf_op jit(solution)/shard_map/cond/branch_0_fun/ppermute | solution.py:335
  28.2 1.1 %collective-permute-done.2.refs_3_ = bf16[128,384]{1,0:T(8,128)(2,1)S(1)} collective-permute-done((bf16[128,384]{1,0:T(8,128)(2,1)S(1)}, bf16[128,384]{1,0:T(8,128)(2,1)S(1)}, u32[]{:S(2)}, u32[]{:S(2)}) %collective-permute-start.2) | collective-permute-done | bytes 98336 | tf_op jit(solution)/shard_map/cond/branch_0_fun/ppermute | solution.py:335
  29.3 0.8 %branch_0_fun.9 = (bf16[384,512]{1,0:T(8,128)(2,1)S(1)}, f32[8,128]{1,0:T(8,128)S(1)}) custom-call(s32[1]{0:T(128)} %get-tuple-element.24.s_ref, bf16[128,384]{1,0:T(8,128)(2,1)S(1)} %get-tuple-element.30.refs_0_, bf16[128,384]{1,0:T(8,128)(2,1)S(1)} %collective-permute-done.refs_1_, bf16[128,384]{1,0:T(8,128)(2,1)S(1)} %collective-permute-done.1.refs_2_, ...), custom_call_target="tpu_custom_call" | custom-call | tf_op jit(solution)/shard_map/cond/branch_0_fun/pallas_call | solution.py:40
  30.2 0.5 %branch_0_fun.11 = (f32[384,768]{1,0:T(8,128)S(1)}, bf16[384,768]{1,0:T(8,128)(2,1)S(1)}) custom-call(f32[8,128]{1,0:T(8,128)S(1)} %get-tuple-element.34.rate_ref, bf16[384,512]{1,0:T(8,128)(2,1)S(1)} %get-tuple-element.35.x_ref, bf16[128,768]{1,0:T(8,128)(2,1)S(1)} %get-tuple-element.39.refs_0_, bf16[128,768]{1,0:T(8,128)(2,1)S(1)} %collective-permute-done.6.refs_1_, ...), custom_call_target="tpu_custom_call" | custom-call | tf_op jit(solution)/shard_map/cond/branch_0_fun/pallas_call | solution.py:40
  30.7 1.0 %collective-permute-start.10 = (bf16[128,256]{1,0:T(8,128)(2,1)S(1)}, bf16[128,256]{1,0:T(8,128)(2,1)S(1)}, u32[]{:S(2)}, u32[]{:S(2)}) collective-permute-start(bf16[128,256]{1,0:T(8,128)(2,1)S(1)} %get-tuple-element.43), channel_id=1, source_target_pairs={{0,1},{1,0},{2,3},{3,2},{4,5},{5,4},{6,7},{7,6},{8,9},{9,8},{10,11... | collective-permute-start | bytes 196616 | tf_op jit(solution)/shard_map/cond/branch_0_fun/ppermute | solution.py:335
  31.7 0.6 %collective-permute-start.11 = (bf16[128,256]{1,0:T(8,128)(2,1)S(1)}, bf16[128,256]{1,0:T(8,128)(2,1)S(1)}, u32[]{:S(2)}, u32[]{:S(2)}) collective-permute-start(bf16[128,256]{1,0:T(8,128)(2,1)S(1)} %get-tuple-element.44), channel_id=1, source_target_pairs={{0,2},{1,3},{2,0},{3,1},{4,6},{5,7},{6,4},{7,5},{8,10},{9,11},{10,... | collective-permute-start | bytes 196616 | tf_op jit(solution)/shard_map/cond/branch_0_fun/ppermute | solution.py:335
  32.3 2.0 %collective-permute-start.12 = (bf16[128,256]{1,0:T(8,128)(2,1)S(1)}, bf16[128,256]{1,0:T(8,128)(2,1)S(1)}, u32[]{:S(2)}, u32[]{:S(2)}) collective-permute-start(bf16[128,256]{1,0:T(8,128)(2,1)S(1)} %get-tuple-element.45), channel_id=1, source_target_pairs={{0,3},{1,2},{2,1},{3,0},{4,7},{5,6},{6,5},{7,4},{8,11},{9,10},{10,... | collective-permute-start | bytes 196616 | tf_op jit(solution)/shard_map/cond/branch_0_fun/ppermute | solution.py:335
  34.3 0.9 %collective-permute-done.10.refs_1_ = bf16[128,256]{1,0:T(8,128)(2,1)S(1)} collective-permute-done((bf16[128,256]{1,0:T(8,128)(2,1)S(1)}, bf16[128,256]{1,0:T(8,128)(2,1)S(1)}, u32[]{:S(2)}, u32[]{:S(2)}) %collective-permute-start.10) | collective-permute-done | bytes 65568 | tf_op jit(solution)/shard_map/cond/branch_0_fun/ppermute | solution.py:335
  35.2 1.4 %collective-permute-done.11.refs_2_ = bf16[128,256]{1,0:T(8,128)(2,1)S(1)} collective-permute-done((bf16[128,256]{1,0:T(8,128)(2,1)S(1)}, bf16[128,256]{1,0:T(8,128)(2,1)S(1)}, u32[]{:S(2)}, u32[]{:S(2)}) %collective-permute-start.11) | collective-permute-done | bytes 65568 | tf_op jit(solution)/shard_map/cond/branch_0_fun/ppermute | solution.py:335
  36.7 0.8 %collective-permute-done.12.refs_3_ = bf16[128,256]{1,0:T(8,128)(2,1)S(1)} collective-permute-done((bf16[128,256]{1,0:T(8,128)(2,1)S(1)}, bf16[128,256]{1,0:T(8,128)(2,1)S(1)}, u32[]{:S(2)}, u32[]{:S(2)}) %collective-permute-start.12) | collective-permute-done | bytes 65568 | tf_op jit(solution)/shard_map/cond/branch_0_fun/ppermute | solution.py:335
  37.5 1.5 %collective-permute-start.13 = (bf16[128,256]{1,0:T(8,128)(2,1)S(1)}, bf16[128,256]{1,0:T(8,128)(2,1)S(1)}, u32[]{:S(2)}, u32[]{:S(2)}) collective-permute-start(bf16[128,256]{1,0:T(8,128)(2,1)S(1)} %branch_0_fun.12.refs_0_.g_ref), channel_id=1, source_target_pairs={{0,2},{1,3},{2,0},{3,1},{4,6},{5,7},{6,4},{7,5},{8,10},{9,11},{10,... | collective-permute-start | bytes 196616 | tf_op jit(solution)/shard_map/cond/branch_0_fun/ppermute | solution.py:335
  39.0 1.1 %collective-permute-start.14 = (bf16[128,256]{1,0:T(8,128)(2,1)S(1)}, bf16[128,256]{1,0:T(8,128)(2,1)S(1)}, u32[]{:S(2)}, u32[]{:S(2)}) collective-permute-start(bf16[128,256]{1,0:T(8,128)(2,1)S(1)} %branch_0_fun.12.refs_0_.g_ref), channel_id=1, source_target_pairs={{0,3},{1,2},{2,1},{3,0},{4,7},{5,6},{6,5},{7,4},{8,11},{9,10},{10,... | collective-permute-start | bytes 196616 | tf_op jit(solution)/shard_map/cond/branch_0_fun/ppermute | solution.py:335
  40.1 1.0 %collective-permute-start.15 = (bf16[128,256]{1,0:T(8,128)(2,1)S(1)}, bf16[128,256]{1,0:T(8,128)(2,1)S(1)}, u32[]{:S(2)}, u32[]{:S(2)}) collective-permute-start(bf16[128,256]{1,0:T(8,128)(2,1)S(1)} %branch_0_fun.12.refs_0_.g_ref), channel_id=1, source_target_pairs={{0,1},{1,0},{2,3},{3,2},{4,5},{5,4},{6,7},{7,6},{8,9},{9,8},{10,11... | collective-permute-start | bytes 196616 | tf_op jit(solution)/shard_map/cond/branch_0_fun/ppermute | solution.py:335
  41.1 1.3 %collective-permute-done.13.refs_1_ = bf16[128,256]{1,0:T(8,128)(2,1)S(1)} collective-permute-done((bf16[128,256]{1,0:T(8,128)(2,1)S(1)}, bf16[128,256]{1,0:T(8,128)(2,1)S(1)}, u32[]{:S(2)}, u32[]{:S(2)}) %collective-permute-start.13) | collective-permute-done | bytes 65568 | tf_op jit(solution)/shard_map/cond/branch_0_fun/ppermute | solution.py:335
  42.3 1.8 %collective-permute-done.14.refs_2_ = bf16[128,256]{1,0:T(8,128)(2,1)S(1)} collective-permute-done((bf16[128,256]{1,0:T(8,128)(2,1)S(1)}, bf16[128,256]{1,0:T(8,128)(2,1)S(1)}, u32[]{:S(2)}, u32[]{:S(2)}) %collective-permute-start.14) | collective-permute-done | bytes 65568 | tf_op jit(solution)/shard_map/cond/branch_0_fun/ppermute | solution.py:335
  44.7 0.9 %branch_0_fun.15.part_ref = f32[128,1536]{1,0:T(8,128)S(1)} custom-call(bf16[128,768]{1,0:T(8,128)(2,1)S(1)} %get-tuple-element.39.refs_0_, bf16[1536,1024]{1,0:T(8,128)(2,1)S(1)} %bitcast.20), custom_call_target="tpu_custom_call" | custom-call | tf_op jit(solution)/shard_map/cond/branch_0_fun/pallas_call | solution.py:40
  45.6 1.1 %input_gradient.3 = bf16[128,1536]{1,0:T(8,128)(2,1)} custom-call(f32[128,1536]{1,0:T(8,128)S(1)} %branch_0_fun.15.part_ref, bf16[128,256]{1,0:T(8,128)(2,1)S(1)} %branch_0_fun.12.refs_0_.g_ref, bf16[1536,1024]{1,0:T(8,128)(2,1)S(1)} %bitcast.21), custom_call_target="tpu_custom_call" | custom-call | tf_op jit(solution)/shard_map/cond/branch_0_fun/input_gradient/pallas_call | solution.py:306
  46.8 1.2 %branch_0_fun.14 = f32[384,1024]{1,0:T(8,128)} custom-call(f32[384,768]{1,0:T(8,128)S(1)} %get-tuple-element.40.refs_0_, bf16[384,768]{1,0:T(8,128)(2,1)S(1)} %collective-permute-done.9.refs_1_, f32[384,256]{1,0:T(8,128)S(1)} %get-tuple-element.46.refs_2_, bf16[384,256]{1,0:T(8,128)(2,1)S(1)} %collective-permute-done.16.refs_3_), custom_call_target="tpu_custom_call" | custom-call | tf_op jit(solution)/shard_map/cond/branch_0_fun/pallas_call | solution.py:248
  (17 shorter events, 0.7 us)
Async XLA Ops:
  1.3 6.3 %copy-start = (bf16[1,1536,1024]{2,1,0:T(8,128)(2,1)S(1)}, bf16[1,1536,1024]{2,1,0:T(8,128)(2,1)}, u32[]{:S(2)}) copy-start(bf16[1,1536,1024]{2,1,0:T(8,128)(2,1)} %get-tuple-element.133) | copy-start | bytes 9437188 | tf_op jit(solution)/shard_map/cond
  3.0 7.2 %collective-permute-start.3 = (bf16[128,256]{1,0:T(8,128)(2,1)S(1)}, bf16[128,256]{1,0:T(8,128)(2,1)S(1)}, u32[]{:S(2)}, u32[]{:S(2)}) collective-permute-start(bf16[128,256]{1,0:T(8,128)(2,1)S(1)} %get-tuple-element.38.refs_2_), channel_id=1, source_target_pairs={{0,1},{1,0},{2,3},{3,2},{4,5},{5,4},{6,7},{7,6},{8,9},{9,8},{10,11... | collective-permute-start | bytes 196616 | tf_op jit(solution)/shard_map/cond/branch_0_fun/ppermute | solution.py:335
  6.1 5.2 %collective-permute-start.4 = (bf16[128,256]{1,0:T(8,128)(2,1)S(1)}, bf16[128,256]{1,0:T(8,128)(2,1)S(1)}, u32[]{:S(2)}, u32[]{:S(2)}) collective-permute-start(bf16[128,256]{1,0:T(8,128)(2,1)S(1)} %get-tuple-element.38.refs_2_), channel_id=1, source_target_pairs={{0,2},{1,3},{2,0},{3,1},{4,6},{5,7},{6,4},{7,5},{8,10},{9,11},{10,... | collective-permute-start | bytes 196616 | tf_op jit(solution)/shard_map/cond/branch_0_fun/ppermute | solution.py:335
  7.6 5.3 %collective-permute-start.5 = (bf16[128,256]{1,0:T(8,128)(2,1)S(1)}, bf16[128,256]{1,0:T(8,128)(2,1)S(1)}, u32[]{:S(2)}, u32[]{:S(2)}) collective-permute-start(bf16[128,256]{1,0:T(8,128)(2,1)S(1)} %get-tuple-element.38.refs_2_), channel_id=1, source_target_pairs={{0,3},{1,2},{2,1},{3,0},{4,7},{5,6},{6,5},{7,4},{8,11},{9,10},{10,... | collective-permute-start | bytes 196616 | tf_op jit(solution)/shard_map/cond/branch_0_fun/ppermute | solution.py:335
  7.6 5.2 %copy-start.3 = (bf16[1,128,768]{2,1,0:T(8,128)(2,1)S(1)}, bf16[1,128,768]{2,1,0:T(8,128)(2,1)}, u32[]{:S(2)}) copy-start(bf16[1,128,768]{2,1,0:T(8,128)(2,1)} %get-tuple-element.136) | copy-start | bytes 589828 | tf_op jit(solution)/shard_map/cond
  8.1 10.5 %collective-permute-start = (bf16[128,384]{1,0:T(8,128)(2,1)S(1)}, bf16[128,384]{1,0:T(8,128)(2,1)S(1)}, u32[]{:S(2)}, u32[]{:S(2)}) collective-permute-start(bf16[128,384]{1,0:T(8,128)(2,1)S(1)} %get-tuple-element.31), channel_id=1, source_target_pairs={{0,2},{1,3},{2,0},{3,1},{4,6},{5,7},{6,4},{7,5},{8,10},{9,11},{10,... | collective-permute-start | bytes 294920 | tf_op jit(solution)/shard_map/cond/branch_0_fun/ppermute | solution.py:335
  14.7 15.4 %collective-permute-start.6 = (bf16[128,768]{1,0:T(8,128)(2,1)S(1)}, bf16[128,768]{1,0:T(8,128)(2,1)S(1)}, u32[]{:S(2)}, u32[]{:S(2)}) collective-permute-start(bf16[128,768]{1,0:T(8,128)(2,1)S(1)} %get-tuple-element.39.refs_0_), channel_id=1, source_target_pairs={{0,2},{1,3},{2,0},{3,1},{4,6},{5,7},{6,4},{7,5},{8,10},{9,11},{10,... | collective-permute-start | bytes 589832 | tf_op jit(solution)/shard_map/cond/branch_0_fun/ppermute | solution.py:335
  15.4 14.7 %collective-permute-start.7 = (bf16[128,768]{1,0:T(8,128)(2,1)S(1)}, bf16[128,768]{1,0:T(8,128)(2,1)S(1)}, u32[]{:S(2)}, u32[]{:S(2)}) collective-permute-start(bf16[128,768]{1,0:T(8,128)(2,1)S(1)} %get-tuple-element.39.refs_0_), channel_id=1, source_target_pairs={{0,3},{1,2},{2,1},{3,0},{4,7},{5,6},{6,5},{7,4},{8,11},{9,10},{10,... | collective-permute-start | bytes 589832 | tf_op jit(solution)/shard_map/cond/branch_0_fun/ppermute | solution.py:335
  16.8 13.4 %collective-permute-start.8 = (bf16[128,768]{1,0:T(8,128)(2,1)S(1)}, bf16[128,768]{1,0:T(8,128)(2,1)S(1)}, u32[]{:S(2)}, u32[]{:S(2)}) collective-permute-start(bf16[128,768]{1,0:T(8,128)(2,1)S(1)} %get-tuple-element.39.refs_0_), channel_id=1, source_target_pairs={{0,1},{1,0},{2,3},{3,2},{4,5},{5,4},{6,7},{7,6},{8,9},{9,8},{10,11... | collective-permute-start | bytes 589832 | tf_op jit(solution)/shard_map/cond/branch_0_fun/ppermute | solution.py:335
  18.3 10.0 %collective-permute-start.1 = (bf16[128,384]{1,0:T(8,128)(2,1)S(1)}, bf16[128,384]{1,0:T(8,128)(2,1)S(1)}, u32[]{:S(2)}, u32[]{:S(2)}) collective-permute-start(bf16[128,384]{1,0:T(8,128)(2,1)S(1)} %get-tuple-element.32), channel_id=1, source_target_pairs={{0,3},{1,2},{2,1},{3,0},{4,7},{5,6},{6,5},{7,4},{8,11},{9,10},{10,... | collective-permute-start | bytes 294920 | tf_op jit(solution)/shard_map/cond/branch_0_fun/ppermute | solution.py:335
  18.6 10.7 %collective-permute-start.2 = (bf16[128,384]{1,0:T(8,128)(2,1)S(1)}, bf16[128,384]{1,0:T(8,128)(2,1)S(1)}, u32[]{:S(2)}, u32[]{:S(2)}) collective-permute-start(bf16[128,384]{1,0:T(8,128)(2,1)S(1)} %get-tuple-element.33), channel_id=1, source_target_pairs={{0,1},{1,0},{2,3},{3,2},{4,5},{5,4},{6,7},{7,6},{8,9},{9,8},{10,11... | collective-permute-start | bytes 294920 | tf_op jit(solution)/shard_map/cond/branch_0_fun/ppermute | solution.py:335
  30.7 16.1 %collective-permute-start.9 = (bf16[384,768]{1,0:T(8,128)(2,1)S(1)}, bf16[384,768]{1,0:T(8,128)(2,1)S(1)}, u32[]{:S(2)}, u32[]{:S(2)}) collective-permute-start(bf16[384,768]{1,0:T(8,128)(2,1)S(1)} %get-tuple-element.41), channel_id=1, source_target_pairs={{0,4},{4,0},{8,12},{12,8},{16,20},{20,16},{24,28},{28,24},{1,5},{5... | collective-permute-start | bytes 1769480 | tf_op jit(solution)/shard_map/cond/branch_0_fun/ppermute | solution.py:345
  30.7 4.5 %collective-permute-start.10 = (bf16[128,256]{1,0:T(8,128)(2,1)S(1)}, bf16[128,256]{1,0:T(8,128)(2,1)S(1)}, u32[]{:S(2)}, u32[]{:S(2)}) collective-permute-start(bf16[128,256]{1,0:T(8,128)(2,1)S(1)} %get-tuple-element.43), channel_id=1, source_target_pairs={{0,1},{1,0},{2,3},{3,2},{4,5},{5,4},{6,7},{7,6},{8,9},{9,8},{10,11... | collective-permute-start | bytes 196616 | tf_op jit(solution)/shard_map/cond/branch_0_fun/ppermute | solution.py:335
  31.7 5.0 %collective-permute-start.11 = (bf16[128,256]{1,0:T(8,128)(2,1)S(1)}, bf16[128,256]{1,0:T(8,128)(2,1)S(1)}, u32[]{:S(2)}, u32[]{:S(2)}) collective-permute-start(bf16[128,256]{1,0:T(8,128)(2,1)S(1)} %get-tuple-element.44), channel_id=1, source_target_pairs={{0,2},{1,3},{2,0},{3,1},{4,6},{5,7},{6,4},{7,5},{8,10},{9,11},{10,... | collective-permute-start | bytes 196616 | tf_op jit(solution)/shard_map/cond/branch_0_fun/ppermute | solution.py:335
  32.3 5.2 %collective-permute-start.12 = (bf16[128,256]{1,0:T(8,128)(2,1)S(1)}, bf16[128,256]{1,0:T(8,128)(2,1)S(1)}, u32[]{:S(2)}, u32[]{:S(2)}) collective-permute-start(bf16[128,256]{1,0:T(8,128)(2,1)S(1)} %get-tuple-element.45), channel_id=1, source_target_pairs={{0,3},{1,2},{2,1},{3,0},{4,7},{5,6},{6,5},{7,4},{8,11},{9,10},{10,... | collective-permute-start | bytes 196616 | tf_op jit(solution)/shard_map/cond/branch_0_fun/ppermute | solution.py:335
  37.5 4.8 %collective-permute-start.13 = (bf16[128,256]{1,0:T(8,128)(2,1)S(1)}, bf16[128,256]{1,0:T(8,128)(2,1)S(1)}, u32[]{:S(2)}, u32[]{:S(2)}) collective-permute-start(bf16[128,256]{1,0:T(8,128)(2,1)S(1)} %branch_0_fun.12.refs_0_.g_ref), channel_id=1, source_target_pairs={{0,2},{1,3},{2,0},{3,1},{4,6},{5,7},{6,4},{7,5},{8,10},{9,11},{10,... | collective-permute-start | bytes 196616 | tf_op jit(solution)/shard_map/cond/branch_0_fun/ppermute | solution.py:335
  39.0 5.2 %collective-permute-start.14 = (bf16[128,256]{1,0:T(8,128)(2,1)S(1)}, bf16[128,256]{1,0:T(8,128)(2,1)S(1)}, u32[]{:S(2)}, u32[]{:S(2)}) collective-permute-start(bf16[128,256]{1,0:T(8,128)(2,1)S(1)} %branch_0_fun.12.refs_0_.g_ref), channel_id=1, source_target_pairs={{0,3},{1,2},{2,1},{3,0},{4,7},{5,6},{6,5},{7,4},{8,11},{9,10},{10,... | collective-permute-start | bytes 196616 | tf_op jit(solution)/shard_map/cond/branch_0_fun/ppermute | solution.py:335
  40.1 4.3 %collective-permute-start.15 = (bf16[128,256]{1,0:T(8,128)(2,1)S(1)}, bf16[128,256]{1,0:T(8,128)(2,1)S(1)}, u32[]{:S(2)}, u32[]{:S(2)}) collective-permute-start(bf16[128,256]{1,0:T(8,128)(2,1)S(1)} %branch_0_fun.12.refs_0_.g_ref), channel_id=1, source_target_pairs={{0,1},{1,0},{2,3},{3,2},{4,5},{5,4},{6,7},{7,6},{8,9},{9,8},{10,11... | collective-permute-start | bytes 196616 | tf_op jit(solution)/shard_map/cond/branch_0_fun/ppermute | solution.py:335
  44.6 2.1 %collective-permute-start.16 = (bf16[384,256]{1,0:T(8,128)(2,1)S(1)}, bf16[384,256]{1,0:T(8,128)(2,1)S(1)}, u32[]{:S(2)}, u32[]{:S(2)}) collective-permute-start(bf16[384,256]{1,0:T(8,128)(2,1)S(1)} %get-tuple-element.47), channel_id=1, source_target_pairs={{0,4},{4,0},{8,12},{12,8},{16,20},{20,16},{24,28},{28,24},{1,5},{5... | collective-permute-start | bytes 589832 | tf_op jit(solution)/shard_map/cond/branch_0_fun/ppermute | solution.py:345
